TPU v7x, 32 devices: a whole 2x2x4 slice. The times are simulated.
32 devices in a mesh: sec: 4 (over z), tile: 4 (over y, core), role: 2 (over x).
Axes of the slice: x: 2, y: 2, z: 4, core: 2. Of those that a mesh axis runs over, the one named last changes fastest.
Arguments:
- pressure: float32 [32, 256, 8192], P(None, 'sec', ('tile', 'role')), may hold values from -6 to 6
- cell_weight: float32 [8192], P(('tile', 'role')), may hold values from 0.25 to 4
- live_cells: int32 [8], replicated, may hold values from 341 to 1024, as said below
- mode_order: int32 [128], replicated, may hold values from 0 to 127, each once
Outputs:
- gram: float32 [128, 32, 32], P('sec', ('tile', 'role'))
Inputs may be any that keep to these rules, and one draw needn't show every extreme that they name: `live_cells`: at least one tile half is full. `mode_order`: each wavenumber appears once.
All inputs are finite; a program needn't handle non-finite values.
Results may differ from a plain program's by a relative error of at most 0.0003.
Values sent between devices are 32-bit elements; how exact they have to be, the bound alone decides.
A program may use at most 128 MiB of HBM per device.

v0:
```python
import functools
import math

import jax
import jax.numpy as jnp
from jax import lax
from jax.experimental import pallas as pl
from jax.experimental.pallas import tpu as pltpu
from jax.sharding import PartitionSpec as P

MESH = pl.DeviceIdType.MESH
LANES = 128
UNROLL = 4
STAGES = 4
SUB = 8
F32 = jnp.float32
BF16 = jnp.bfloat16


def halves(x):
    hi = x.astype(BF16)
    lo = (x - hi.astype(F32)).astype(BF16)
    return hi, lo


def left_terms(x):
    hi, lo = halves(x)
    return jnp.concatenate([hi, hi, lo], axis=1)


def right_terms(x):
    hi, lo = halves(x)
    return jnp.concatenate([hi, lo, hi], axis=0)


def dot(a, b, dims=(((1,), (0,)), ((), ()))):
    return lax.dot_general(a, b, dims, preferred_element_type=F32)


def partner(x, me, n):
    other, bit = 0, 1
    while bit < n:
        other += (me // bit + x // bit) % 2 * bit
        bit *= 2
    return other


def iota(shape, axis):
    return lax.broadcasted_iota(jnp.int32, shape, axis)


def time_terms(snaps):
    size = snaps * SUB
    row, col = iota((size, size), 0), iota((size, size), 1)
    half = snaps // 2
    r, t = row // SUB, col // SUB
    f = r % half
    hann = 0.5 - 0.5 * jnp.cos((2.0 * math.pi / snaps) * t.astype(F32))
    phase = (2.0 * math.pi / snaps) * ((f * t) % snaps).astype(F32)
    wave = jnp.where(r < half, jnp.cos(phase), -jnp.sin(phase))
    value = math.sqrt(8.0 / (3.0 * snaps)) * hann * wave
    return jnp.where(row % SUB == col % SUB, value, 0.0)


def angle_terms(modes_row, angles, first, count):
    index = first + iota((count, modes_row.shape[1]), 0)
    phase = (2.0 * math.pi / angles) * ((modes_row * index) % angles).astype(F32)
    scale = 1.0 / math.sqrt(angles)
    return jnp.concatenate([(jnp.cos(phase) * scale).T, (jnp.sin(phase) * scale).T], axis=0)


def kernel(n_sec, n_tile, n_role, p_ref, w_ref, live_ref, mode_ref, out_ref,
           recv, spec, zbuf, acc, pbuf, pacc, reda, sb, redb, ttab, atab, ltab, ypart,
           send_sem, recv_sem, own_sem, pa_sem, pr_sem, sa_sem, ra_sem, sb_sem, rb_sem):
    me = lax.axis_index("sec")
    tile, role = lax.axis_index("tile"), lax.axis_index("role")
    n_grp = n_tile * n_role
    grp = tile * n_role + role
    near = n_grp // 2
    side, mine = tile % 2, tile // 2 * n_role + role
    snaps, q_loc, cells = p_ref.shape
    half = snaps // 2
    angles = q_loc * n_sec
    modes = mode_ref.shape[1]
    cell_dev = cells // n_sec
    subs = cell_dev // LANES
    pack = LANES // snaps
    part = snaps // n_grp
    split = q_loc % 16 == 0

    def peer(o):
        other = lax.rem(grp + o, n_grp)
        return other, {"tile": other // n_role, "role": other % n_role}

    barrier = pltpu.get_barrier_semaphore()
    for o in range(1, n_sec):
        pl.semaphore_signal(barrier, inc=1, device_id={"sec": lax.rem(me + o, n_sec)}, device_id_type=MESH)
    for o in range(1, n_grp):
        pl.semaphore_signal(barrier, inc=1, device_id=peer(o)[1], device_id_type=MESH)
    pl.semaphore_wait(barrier, n_sec + n_grp - 2)

    def piece(owner, j):
        start = pl.multiple_of(owner * cell_dev + j * LANES, LANES)
        return p_ref.at[:, :, pl.ds(start, LANES)]

    def outgoing(i, j):
        dest = partner(i, me, n_sec)
        return pltpu.make_async_remote_copy(
            src_ref=piece(dest, j), dst_ref=recv.at[j, me],
            send_sem=send_sem.at[j, dest], recv_sem=recv_sem.at[j, me],
            device_id={"sec": dest}, device_id_type=MESH)

    def own(j):
        return pltpu.make_async_copy(piece(me, j), recv.at[j, me], own_sem.at[j])

    for j in range(subs):
        @pl.loop(1, n_sec)
        def _(i):
            outgoing(i, j).start()
    for j in range(subs):
        own(j).start()

    ttab[...] = left_terms(time_terms(snaps))
    atab[...] = left_terms(angle_terms(mode_ref[...], angles, 0, angles))
    late = partner(n_sec - 1, me, n_sec)
    late_at = pl.multiple_of(late * q_loc, SUB)
    if split:
        ltab[...] = left_terms(angle_terms(mode_ref[...], angles, late_at, q_loc))
    live = live_ref[grp]
    total = float(cells * n_grp)
    wide = 2 if q_loc % (2 * SUB) == 0 else 1

    def to_spectra(j, src):
        for g in range(0, q_loc, wide * SUB):
            x = jnp.concatenate(
                [recv[j, src, :, g + u * SUB:g + (u + 1) * SUB, :].reshape(snaps * SUB, LANES) for u in range(wide)],
                axis=1)
            y = dot(ttab[...], right_terms(x))
            for u in range(wide):
                at = pl.multiple_of(src * q_loc + g + u * SUB, SUB)
                spec[:, pl.ds(at, SUB), :] = y[:, u * LANES:(u + 1) * LANES].reshape(snaps, SUB, LANES)

    stage_rows = acc.shape[1] // STAGES

    def pair(t):
        at = pl.ds(t * stage_rows, stage_rows)
        return pltpu.make_async_remote_copy(
            src_ref=acc.at[pl.ds((1 - side) * near, near), at, :], dst_ref=pbuf.at[:, at, :],
            send_sem=pa_sem.at[t], recv_sem=pr_sem.at[t],
            device_id={"tile": tile + 1 - 2 * side}, device_id_type=MESH)

    def share(o, t, arriving=False):
        other = lax.rem(mine + o, near)
        at = pl.ds(t * stage_rows, stage_rows)
        slot = other if arriving else mine
        return pltpu.make_async_remote_copy(
            src_ref=pacc.at[other, at, :], dst_ref=reda.at[slot, at, :],
            send_sem=sa_sem.at[t, other], recv_sem=ra_sem.at[t, slot],
            device_id={"tile": other // n_role * 2 + side, "role": other % n_role}, device_id_type=MESH)

    def forward(t):
        pair(t).wait_recv()
        at = pl.ds(t * stage_rows, stage_rows)
        pacc[:, at, :] = acc[pl.ds(side * near, near), at, :] + pbuf[:, at, :]
        for o in range(1, near):
            share(o, t).start()

    def arrive(i, j):
        src = partner(i, me, n_sec)
        pltpu.make_async_remote_copy(
            src_ref=recv.at[j, src], dst_ref=recv.at[j, src],
            send_sem=send_sem.at[j, src], recv_sem=recv_sem.at[j, src],
            device_id={"sec": src}, device_id_type=MESH).wait_recv()
        to_spectra(j, src)

    def to_modal(f, y):
        zbuf[pl.ds(f, modes, stride=snaps), :] = y[:modes, :LANES] + y[modes:, LANES:]
        zbuf[pl.ds(half + f, modes, stride=snaps), :] = y[:modes, LANES:] - y[modes:, :LANES]

    def products(f):
        x = jnp.concatenate([spec[f], spec[half + f]], axis=1)
        return dot(atab[...], right_terms(x))

    for j in range(subs):
        own(j).wait()
        to_spectra(j, me)
        early = split and j == subs - 1

        @pl.loop(1, n_sec - 1 if early else n_sec)
        def _(i):
            arrive(i, j)

        if early:
            spec[:, pl.ds(late_at, q_loc), :] = jnp.zeros((snaps, q_loc, LANES), F32)

            @pl.loop(0, half)
            def _(f):
                ypart[f] = products(f)

            arrive(n_sec - 1, j)

            @pl.loop(0, half, unroll=UNROLL)
            def _(f):
                x = jnp.concatenate([spec[f, pl.ds(late_at, q_loc), :], spec[half + f, pl.ds(late_at, q_loc), :]], axis=1)
                to_modal(f, ypart[f] + dot(ltab[...], right_terms(x)))
        else:
            @pl.loop(0, half, unroll=UNROLL)
            def _(f):
                to_modal(f, products(f))

        first = pl.multiple_of(me * cell_dev + j * LANES, LANES)
        position = first + iota((1, LANES), 1)
        weight = jnp.where(position < live, w_ref[pl.ds(me * subs + j, 1), :] / total, 0.0)
        block = iota((snaps, LANES), 1) // snaps
        steps = SUB // part

        def gram(h):
            rows = []
            for u in range(steps):
                at = pl.multiple_of((h * steps + u) * LANES, LANES)
                z = zbuf[pl.ds(at, LANES), :]
                zh, zl = halves(z)
                g4 = dot(left_terms(z * weight), jnp.concatenate([zh, zl, zh], axis=1), (((1,), (1,)), ((), ())))
                r = g4[:snaps]
                for b in range(1, pack):
                    r = jnp.where(block == b, g4[b * snaps:(b + 1) * snaps], r)
                rows.append(r)
            at = pl.multiple_of(h * SUB, SUB)
            for g in range(n_grp):
                new = jnp.concatenate([r[g * part:(g + 1) * part] for r in rows], axis=0)
                to = g // n_role % 2 * near + g // n_role // 2 * n_role + g % n_role
                if j == 0:
                    acc[to, pl.ds(at, SUB), :] = new
                else:
                    acc[to, pl.ds(at, SUB), :] += new

        count = modes // pack // steps // STAGES
        for t in range(STAGES):
            pl.loop(t * count, (t + 1) * count, unroll=UNROLL)(gram)
            if j == subs - 1:
                pair(t).start()
                if t > 0:
                    forward(t - 1)

    def last(s, slot):
        return pltpu.make_async_remote_copy(
            src_ref=sb.at[s], dst_ref=redb.at[slot],
            send_sem=sb_sem.at[s], recv_sem=rb_sem.at[slot],
            device_id={"sec": s}, device_id_type=MESH)

    forward(STAGES - 1)
    rows = sb.shape[1]
    for t in range(STAGES):
        for o in range(1, near):
            share(o, t, True).wait_recv()
        for s in range(t * n_sec // STAGES, (t + 1) * n_sec // STAGES):
            value = pacc[mine, s * rows:(s + 1) * rows, :]
            for o in range(1, near):
                value += reda[lax.rem(mine + o, near), s * rows:(s + 1) * rows, :]
            sb[s] = value

            @pl.when(me != s)
            def _():
                last(s, me).start()

    value = sb[me]
    for o in range(1, n_sec):
        s = lax.rem(me + o, n_sec)
        last(s, s).wait_recv()
        value += redb[s]
    out_ref[...] = value

    for j in range(subs):
        @pl.loop(1, n_sec)
        def _(i):
            outgoing(i, j).wait_send()
    for t in range(STAGES):
        pair(t).wait_send()
        for o in range(1, near):
            share(o, t).wait_send()
    for o in range(1, n_sec):
        last(lax.rem(me + o, n_sec), me).wait_send()


def on_device(pressure, cell_weight, live_cells, mode_order):
    n_sec, n_tile, n_role = (lax.axis_size(a) for a in ("sec", "tile", "role"))
    n_grp = n_tile * n_role
    snaps, q_loc, cells = pressure.shape
    modes = mode_order.shape[0]
    angles = q_loc * n_sec
    subs = cells // n_sec // LANES
    pack = LANES // snaps
    part = snaps // n_grp
    rows = modes // pack * part
    own_rows = rows // n_sec
    vmem = pl.BlockSpec(memory_space=pltpu.VMEM)
    dma = pltpu.SemaphoreType.DMA
    packed = pl.pallas_call(
        functools.partial(kernel, n_sec, n_tile, n_role),
        out_shape=jax.ShapeDtypeStruct((own_rows, LANES), F32),
        in_specs=[pl.BlockSpec(memory_space=pl.ANY), vmem, pl.BlockSpec(memory_space=pltpu.SMEM), vmem],
        out_specs=vmem,
        scratch_shapes=[
            pltpu.VMEM((subs, n_sec, snaps, q_loc, LANES), F32),
            pltpu.VMEM((snaps, angles, LANES), F32),
            pltpu.VMEM((modes * snaps, LANES), F32),
            pltpu.VMEM((n_grp, rows, LANES), F32),
            pltpu.VMEM((n_grp // 2, rows, LANES), F32),
            pltpu.VMEM((n_grp // 2, rows, LANES), F32),
            pltpu.VMEM((n_grp // 2, rows, LANES), F32),
            pltpu.VMEM((n_sec, own_rows, LANES), F32),
            pltpu.VMEM((n_sec, own_rows, LANES), F32),
            pltpu.VMEM((snaps * SUB, 3 * snaps * SUB), BF16),
            pltpu.VMEM((2 * modes, 3 * angles), BF16),
            pltpu.VMEM((2 * modes, 3 * q_loc), BF16),
            pltpu.VMEM((snaps // 2, 2 * modes, 2 * LANES), F32),
            dma((subs, n_sec)), dma((subs, n_sec)), dma((subs,)),
            dma((STAGES,)), dma((STAGES,)), dma((STAGES, n_grp // 2)), dma((STAGES, n_grp // 2)), dma((n_sec,)), dma((n_sec,)),
        ],
        compiler_params=pltpu.CompilerParams(
            collective_id=0, has_side_effects=True, vmem_limit_bytes=60 * 2**20),
        name="spod",
    )(pressure, cell_weight.reshape(cells // LANES, LANES), live_cells, mode_order.reshape(1, modes))
    out = packed.reshape(modes // pack // n_sec, part, pack, snaps)
    return out.transpose(0, 2, 1, 3).reshape(modes // n_sec, part, snaps)


def solution(mesh):
    in_specs = (P(None, "sec", ("tile", "role")), P(("tile", "role")), P(), P())
    out_specs = P("sec", ("tile", "role"), None)
    return jax.shard_map(
        on_device, mesh=mesh, in_specs=in_specs, out_specs=out_specs, check_vma=False
    )
```

profile of v0, /device:TPU:0, one launch (start us, length us, event | category | flops | bytes accessed | tf_op | source)
XLA Modules:
  0.0 201.6 jit_solution(9962505560167518558)
XLA Ops:
  0.0 200.1 %spod.1 = f32[32,128]{1,0:T(8,128)} custom-call(f32[32,64,1024]{2,1,0:T(8,128)} %p_ref.1, f32[8,128]{1,0:T(8,128)} %bitcast.5, s32[8]{0:T(128)} %live_ref.1, s32[1,128]{1,0:T(1,128)} %bitcast.6), custom_call_target="tpu_custom_call" | custom-call | tf_op jit(solution)/shard_map/spod/pallas_call | solution.py:298
  200.1 0.8 reshape.14
  201.0 0.6 copy.5
where the time goes:
time: 202 us
  Pallas kernels  200 us (99%)
    pallas_call x1, Pallas kernels, on_device(): pl.pallas_call(functools.partial(kernel, n_sec, n_tile, n_role), out_shap...  200 us

commit v1 on v0

--- a/solution.py
+++ b/solution.py
@@ -282,25 +282,432 @@
         last(lax.rem(me + o, n_sec), me).wait_send()
 
 
+def flip(x, bit):
+    return x + bit - 2 * bit * (x // bit % 2)
+
+
+def slot_table(slots, n_sec, subs):
+    half = n_sec // 2
+    table = [None] * slots
+    for right in (1, 0):
+        mine = range(1 - right, slots, 2)
+        pad = subs * half - len(mine)
+        for i, j in enumerate(mine):
+            at = half - 1 - (i + pad) % half
+            table[j] = (half + at if right else half - 1 - at, (i + pad) // half)
+    return table
+
+
+def ragged(slots, floor, n_sec, n_tile, n_role, *refs):
+    n_grp = n_tile * n_role
+    near = n_grp // 2
+    (p_ref, w_ref, live_ref, mode_ref, out_ref,
+     recv, spec, zbuf, acc, pbuf, pacc, reda, sb, redb, ttab, atab, ltab, ypart,
+     send_sem, recv_sem, own_sem, pa_sem, pr_sem, sa_sem, ra_sem, sb_sem, rb_sem) = refs[:27]
+    extra = refs[27:]
+    me = lax.axis_index("sec")
+    tile, role = lax.axis_index("tile"), lax.axis_index("role")
+    grp = tile * n_role + role
+    side, mine = tile % 2, tile // 2 * n_role + role
+    snaps, q_loc, cells = p_ref.shape
+    half = snaps // 2
+    angles = q_loc * n_sec
+    modes = mode_ref.shape[1]
+    blocks = cells // LANES
+    subs = recv.shape[0]
+    pack = LANES // snaps
+    part = snaps // n_grp
+    spare = blocks - slots
+    fixed = floor if spare else slots
+    table = slot_table(slots, n_sec, subs)
+    core, xbit, ybit = n_role, 1, 2 * n_role
+    if spare:
+        pools, stage, wall, home_sem, keep_sem, ls_sem, lr_sem, ws_sem, wr_sem = (
+            extra[:spare], *extra[spare:])
+
+    def at_plane(g):
+        return {"tile": g // n_role, "role": g % n_role}
+
+    barrier = pltpu.get_barrier_semaphore()
+    for o in range(1, n_sec):
+        pl.semaphore_signal(barrier, inc=1, device_id={"sec": lax.rem(me + o, n_sec)}, device_id_type=MESH)
+    for o in range(1, n_grp):
+        pl.semaphore_signal(barrier, inc=1, device_id=at_plane(lax.rem(grp + o, n_grp)), device_id_type=MESH)
+    pl.semaphore_wait(barrier, n_sec + n_grp - 2)
+
+    def piece(j):
+        return p_ref.at[:, :, pl.ds(j * LANES, LANES)]
+
+    def content(j):
+        return piece(j) if j < fixed else stage.at[j - fixed]
+
+    def owner(j):
+        z = table[j][0]
+        return z + side * (n_sec - 1 - 2 * z)
+
+    def outgoing(j):
+        sub = table[j][1]
+        return pltpu.make_async_remote_copy(
+            src_ref=content(j), dst_ref=recv.at[sub, me],
+            send_sem=send_sem.at[j], recv_sem=recv_sem.at[sub, me],
+            device_id={"sec": owner(j)}, device_id_type=MESH)
+
+    def own(j):
+        sub = table[j][1]
+        return pltpu.make_async_copy(content(j), recv.at[sub, me], own_sem.at[sub])
+
+    def is_far(j):
+        return owner(j) // (n_sec // 2) != me // (n_sec // 2)
+
+    def launch(js):
+        for j in js:
+            @pl.when(is_far(j))
+            def _():
+                outgoing(j).start()
+        for j in js:
+            @pl.when(jnp.logical_and(jnp.logical_not(is_far(j)), owner(j) != me))
+            def _():
+                outgoing(j).start()
+
+            @pl.when(owner(j) == me)
+            def _():
+                own(j).start()
+
+    launch(range(fixed))
+
+    count = [jnp.maximum((live_ref[g] + (LANES - 1)) // LANES, fixed) for g in range(n_grp)]
+
+    def plan(j):
+        mine_count = jnp.int32(0)
+        want = jnp.int32(0)
+        for g in range(n_grp):
+            mine_count += jnp.where(grp == g, count[g], 0)
+            for k in range(fixed, slots):
+                want += jnp.where(jnp.logical_and(k < j, count[g] <= k), 1, 0)
+            want += jnp.where(jnp.logical_and(g < grp, count[g] <= j), 1, 0)
+        home = j < mine_count
+        seen = jnp.int32(0)
+        from_g, from_k, found = jnp.int32(0), jnp.int32(0), jnp.int32(0)
+        for k in range(spare):
+            for g in range(n_grp):
+                has = jnp.where(count[g] > slots + k, 1, 0)
+                hit = jnp.where(seen == want, has, 0)
+                from_g += hit * g
+                from_k += hit * k
+                found += hit
+                seen += has
+        return home, found, from_g, from_k
+
+    if spare:
+        gx, gy, gc = flip(grp, xbit), flip(grp, ybit), flip(grp, core)
+        gxy = flip(gx, ybit)
+        offset = slots - fixed
+
+        def place(k, g):
+            return pools[k].at[g + (offset if k == 0 else 0)]
+
+        def pass_on(k, n, origin, to):
+            src = piece(slots + k) if origin is grp else place(k, origin)
+            return pltpu.make_async_remote_copy(
+                src_ref=src, dst_ref=place(k, origin),
+                send_sem=ls_sem.at[k, n], recv_sem=lr_sem.at[k, origin],
+                device_id=at_plane(to), device_id_type=MESH)
+
+        hops = [(grp, gx), (grp, gy), (grp, gc), (gx, gy), (gx, gc), (gy, gc), (gxy, gc)]
+
+        def hop(k, n):
+            return pass_on(k, n, *hops[n])
+
+        def came(k, origin):
+            pltpu.make_async_remote_copy(
+                src_ref=place(k, origin), dst_ref=place(k, origin),
+                send_sem=ls_sem.at[k, 0], recv_sem=lr_sem.at[k, origin],
+                device_id=at_plane(gx), device_id_type=MESH).wait_recv()
+
+        def keep(k):
+            return pltpu.make_async_copy(piece(slots + k), place(k, grp), keep_sem.at[k])
+
+        def hold(j):
+            return pltpu.make_async_copy(piece(j), pools[0].at[j - fixed], home_sem.at[j - fixed])
+
+        def weight_to(o):
+            return pltpu.make_async_remote_copy(
+                src_ref=w_ref, dst_ref=wall.at[grp],
+                send_sem=ws_sem.at[o], recv_sem=wr_sem.at[grp],
+                device_id=at_plane(lax.rem(grp + o, n_grp)), device_id_type=MESH)
+
+        def weight_from(o):
+            other = lax.rem(grp + o, n_grp)
+            return pltpu.make_async_remote_copy(
+                src_ref=w_ref, dst_ref=wall.at[other],
+                send_sem=ws_sem.at[o], recv_sem=wr_sem.at[other],
+                device_id=at_plane(other), device_id_type=MESH)
+
+        for k in range(spare):
+            for n in (0, 1, 2) if k == 0 else (0, 2):
+                hop(k, n).start()
+        for j in range(fixed, slots):
+            hold(j).start()
+        for k in range(spare):
+            keep(k).start()
+        for o in range(1, n_grp):
+            weight_to(o).start()
+        wall[grp] = w_ref[...]
+
+    acc[...] = jnp.zeros(acc.shape, F32)
+    ttab[...] = left_terms(time_terms(snaps))
+    atab[...] = left_terms(angle_terms(mode_ref[...], angles, 0, angles))
+    late = partner(n_sec - 1, me, n_sec)
+    late_at = pl.multiple_of(late * q_loc, SUB)
+    ltab[...] = left_terms(angle_terms(mode_ref[...], angles, late_at, q_loc))
+    total = float(cells * n_grp)
+
+    if spare:
+        def fill(j):
+            home, found, from_g, from_k = plan(j)
+            foreign = jnp.where(home, 0, found)
+            first = jnp.where(jnp.logical_and(foreign == 1, from_k == 0), from_g + offset, j - fixed)
+            second = jnp.where(jnp.logical_and(foreign == 1, from_k == 1), 1, 0)
+            both = spare > 1 and j > fixed
+
+            @pl.loop(0, snaps, unroll=UNROLL)
+            def _(t):
+                x = pools[0][first, t]
+                if both:
+                    x = jnp.where(second == 1, pools[1][from_g, t], x)
+                stage[j - fixed, t] = x
+
+        for k in range(spare):
+            came(k, gx)
+            hop(k, 3).start()
+            hop(k, 4).start()
+            if k + 1 < spare:
+                hop(k + 1, 1).start()
+            came(k, gy)
+            hop(k, 5).start()
+            came(k, gxy)
+            hop(k, 6).start()
+            for g in (gc, flip(gx, core), flip(gy, core), flip(gxy, core)):
+                came(k, g)
+            keep(k).wait()
+            if k == 0:
+                for j in range(fixed, slots):
+                    hold(j).wait()
+            js = range(fixed, slots) if spare == 1 else (range(fixed, fixed + 1) if k == 0 else range(fixed + 1, slots))
+            for j in js:
+                fill(j)
+                launch([j])
+        for o in range(1, n_grp):
+            weight_from(o).wait_recv()
+
+    rank = me + side * (n_sec - 1 - 2 * me)
+
+    def holding(sub):
+        slot, have = jnp.int32(0), jnp.int32(0)
+        for j, (z, s) in enumerate(table):
+            if s == sub:
+                slot += jnp.where(rank == z, j, 0)
+                have += jnp.where(rank == z, 1, 0)
+        return slot, have
+
+    def weight_row(sub):
+        slot, _ = holding(sub)
+        lane = iota((1, LANES), 1)
+        row = iota((blocks, LANES), 0)
+        if spare:
+            home, found, from_g, from_k = plan(slot)
+            g = jnp.where(home, grp, from_g)
+            b = jnp.where(home, slot, slots + from_k)
+            used = jnp.where(home, 1, found)
+            live = jnp.int32(0)
+            w = jnp.zeros((1, LANES), F32)
+            for h in range(n_grp):
+                live += jnp.where(g == h, live_ref[h], 0)
+                w += jnp.sum(jnp.where(row == jnp.where(g == h, b, -1), wall[h], 0.0), axis=0, keepdims=True)
+            live = jnp.where(used == 1, live, 0)
+        else:
+            b, live = slot, live_ref[grp]
+            w = jnp.sum(jnp.where(row == b, w_ref[...], 0.0), axis=0, keepdims=True)
+        return jnp.where(b * LANES + lane < live, w / total, 0.0)
+
+    wide = 2
+
+    def to_spectra(j, src):
+        for g in range(0, q_loc, wide * SUB):
+            x = jnp.concatenate(
+                [recv[j, src, :, g + u * SUB:g + (u + 1) * SUB, :].reshape(snaps * SUB, LANES) for u in range(wide)],
+                axis=1)
+            y = dot(ttab[...], right_terms(x))
+            for u in range(wide):
+                at = pl.multiple_of(src * q_loc + g + u * SUB, SUB)
+                spec[:, pl.ds(at, SUB), :] = y[:, u * LANES:(u + 1) * LANES].reshape(snaps, SUB, LANES)
+
+    stage_rows = acc.shape[1] // STAGES
+
+    def pair(t):
+        at = pl.ds(t * stage_rows, stage_rows)
+        return pltpu.make_async_remote_copy(
+            src_ref=acc.at[pl.ds((1 - side) * near, near), at, :], dst_ref=pbuf.at[:, at, :],
+            send_sem=pa_sem.at[t], recv_sem=pr_sem.at[t],
+            device_id={"tile": tile + 1 - 2 * side}, device_id_type=MESH)
+
+    def share(o, t, arriving=False):
+        other = lax.rem(mine + o, near)
+        at = pl.ds(t * stage_rows, stage_rows)
+        slot = other if arriving else mine
+        return pltpu.make_async_remote_copy(
+            src_ref=pacc.at[other, at, :], dst_ref=reda.at[slot, at, :],
+            send_sem=sa_sem.at[t, other], recv_sem=ra_sem.at[t, slot],
+            device_id={"tile": other // n_role * 2 + side, "role": other % n_role}, device_id_type=MESH)
+
+    def forward(t):
+        pair(t).wait_recv()
+        at = pl.ds(t * stage_rows, stage_rows)
+        pacc[:, at, :] = acc[pl.ds(side * near, near), at, :] + pbuf[:, at, :]
+        for o in range(1, near):
+            share(o, t).start()
+
+    def arrive(i, j):
+        src = partner(i, me, n_sec)
+        pltpu.make_async_remote_copy(
+            src_ref=recv.at[j, src], dst_ref=recv.at[j, src],
+            send_sem=send_sem.at[j], recv_sem=recv_sem.at[j, src],
+            device_id={"sec": src}, device_id_type=MESH).wait_recv()
+        to_spectra(j, src)
+
+    def to_modal(f, y):
+        zbuf[pl.ds(f, modes, stride=snaps), :] = y[:modes, :LANES] + y[modes:, LANES:]
+        zbuf[pl.ds(half + f, modes, stride=snaps), :] = y[:modes, LANES:] - y[modes:, :LANES]
+
+    def products(f):
+        x = jnp.concatenate([spec[f], spec[half + f]], axis=1)
+        return dot(atab[...], right_terms(x))
+
+    def process(j):
+        early = j == subs - 1
+        pltpu.make_async_copy(piece(0), recv.at[j, me], own_sem.at[j]).wait()
+        to_spectra(j, me)
+
+        @pl.loop(1, n_sec - 1 if early else n_sec)
+        def _(i):
+            arrive(i, j)
+
+        if early:
+            spec[:, pl.ds(late_at, q_loc), :] = jnp.zeros((snaps, q_loc, LANES), F32)
+
+            @pl.loop(0, half)
+            def _(f):
+                ypart[f] = products(f)
+
+            arrive(n_sec - 1, j)
+
+            @pl.loop(0, half, unroll=UNROLL)
+            def _(f):
+                x = jnp.concatenate([spec[f, pl.ds(late_at, q_loc), :], spec[half + f, pl.ds(late_at, q_loc), :]], axis=1)
+                to_modal(f, ypart[f] + dot(ltab[...], right_terms(x)))
+        else:
+            @pl.loop(0, half, unroll=UNROLL)
+            def _(f):
+                to_modal(f, products(f))
+
+        weight = weight_row(j)
+        block = iota((snaps, LANES), 1) // snaps
+        steps = SUB // part
+
+        def gram(h):
+            rows = []
+            for u in range(steps):
+                at = pl.multiple_of((h * steps + u) * LANES, LANES)
+                z = zbuf[pl.ds(at, LANES), :]
+                zh, zl = halves(z)
+                g4 = dot(left_terms(z * weight), jnp.concatenate([zh, zl, zh], axis=1), (((1,), (1,)), ((), ())))
+                r = g4[:snaps]
+                for b in range(1, pack):
+                    r = jnp.where(block == b, g4[b * snaps:(b + 1) * snaps], r)
+                rows.append(r)
+            at = pl.multiple_of(h * SUB, SUB)
+            for g in range(n_grp):
+                new = jnp.concatenate([r[g * part:(g + 1) * part] for r in rows], axis=0)
+                to = g // n_role % 2 * near + g // n_role // 2 * n_role + g % n_role
+                acc[to, pl.ds(at, SUB), :] += new
+
+        size = modes // pack // steps // STAGES
+        for t in range(STAGES):
+            pl.loop(t * size, (t + 1) * size, unroll=UNROLL)(gram)
+            if early:
+                pair(t).start()
+                if t > 0:
+                    forward(t - 1)
+
+    for j in range(subs - 1):
+        pl.when(holding(j)[1] == 1)(functools.partial(process, j))
+    process(subs - 1)
+
+    def last(s, slot):
+        return pltpu.make_async_remote_copy(
+            src_ref=sb.at[s], dst_ref=redb.at[slot],
+            send_sem=sb_sem.at[s], recv_sem=rb_sem.at[slot],
+            device_id={"sec": s}, device_id_type=MESH)
+
+    forward(STAGES - 1)
+    rows = sb.shape[1]
+    for t in range(STAGES):
+        for o in range(1, near):
+            share(o, t, True).wait_recv()
+        for s in range(t * n_sec // STAGES, (t + 1) * n_sec // STAGES):
+            value = pacc[mine, s * rows:(s + 1) * rows, :]
+            for o in range(1, near):
+                value += reda[lax.rem(mine + o, near), s * rows:(s + 1) * rows, :]
+            sb[s] = value
+
+            @pl.when(me != s)
+            def _():
+                last(s, me).start()
+
+    value = sb[me]
+    for o in range(1, n_sec):
+        s = lax.rem(me + o, n_sec)
+        last(s, s).wait_recv()
+        value += redb[s]
+    out_ref[...] = value
+
+    for j in range(slots):
+        @pl.when(owner(j) != me)
+        def _():
+            outgoing(j).wait_send()
+    if spare:
+        for k in range(spare):
+            for n in range(len(hops)):
+                hop(k, n).wait_send()
+        for o in range(1, n_grp):
+            weight_to(o).wait_send()
+    for t in range(STAGES):
+        pair(t).wait_send()
+        for o in range(1, near):
+            share(o, t).wait_send()
+    for o in range(1, n_sec):
+        last(lax.rem(me + o, n_sec), me).wait_send()
+
+
 def on_device(pressure, cell_weight, live_cells, mode_order):
     n_sec, n_tile, n_role = (lax.axis_size(a) for a in ("sec", "tile", "role"))
     n_grp = n_tile * n_role
     snaps, q_loc, cells = pressure.shape
     modes = mode_order.shape[0]
     angles = q_loc * n_sec
-    subs = cells // n_sec // LANES
+    blocks = cells // LANES
+    subs = blocks // n_sec
     pack = LANES // snaps
     part = snaps // n_grp
     rows = modes // pack * part
     own_rows = rows // n_sec
     vmem = pl.BlockSpec(memory_space=pltpu.VMEM)
     dma = pltpu.SemaphoreType.DMA
-    packed = pl.pallas_call(
-        functools.partial(kernel, n_sec, n_tile, n_role),
-        out_shape=jax.ShapeDtypeStruct((own_rows, LANES), F32),
-        in_specs=[pl.BlockSpec(memory_space=pl.ANY), vmem, pl.BlockSpec(memory_space=pltpu.SMEM), vmem],
-        out_specs=vmem,
-        scratch_shapes=[
+    adaptive = subs == 2 and n_grp == blocks and n_role == 2 and n_sec == 4 and q_loc % 16 == 0
+    floor = -(-(cells // 3) // LANES)
+
+    def scratch(slots):
+        shapes = [
             pltpu.VMEM((subs, n_sec, snaps, q_loc, LANES), F32),
             pltpu.VMEM((snaps, angles, LANES), F32),
             pltpu.VMEM((modes * snaps, LANES), F32),
@@ -314,13 +721,46 @@
             pltpu.VMEM((2 * modes, 3 * angles), BF16),
             pltpu.VMEM((2 * modes, 3 * q_loc), BF16),
             pltpu.VMEM((snaps // 2, 2 * modes, 2 * LANES), F32),
-            dma((subs, n_sec)), dma((subs, n_sec)), dma((subs,)),
+            dma((slots,) if adaptive else (subs, n_sec)), dma((subs, n_sec)), dma((subs,)),
             dma((STAGES,)), dma((STAGES,)), dma((STAGES, n_grp // 2)), dma((STAGES, n_grp // 2)), dma((n_sec,)), dma((n_sec,)),
-        ],
-        compiler_params=pltpu.CompilerParams(
-            collective_id=0, has_side_effects=True, vmem_limit_bytes=60 * 2**20),
-        name="spod",
-    )(pressure, cell_weight.reshape(cells // LANES, LANES), live_cells, mode_order.reshape(1, modes))
+        ]
+        spare = blocks - slots
+        if adaptive and spare:
+            block = (snaps, q_loc, LANES)
+            extra = slots - floor
+            shapes += [pltpu.VMEM((n_grp + (extra if k == 0 else 0), *block), F32) for k in range(spare)]
+            shapes += [
+                pltpu.VMEM((extra, *block), F32),
+                pltpu.VMEM((n_grp, blocks, LANES), F32),
+                dma((extra,)), dma((spare,)), dma((spare, n_grp)), dma((spare, n_grp)), dma((n_grp,)), dma((n_grp,)),
+            ]
+        return shapes
+
+    def call(slots):
+        body = functools.partial(ragged, slots, floor) if adaptive else kernel
+        return pl.pallas_call(
+            functools.partial(body, n_sec, n_tile, n_role),
+            out_shape=jax.ShapeDtypeStruct((own_rows, LANES), F32),
+            in_specs=[pl.BlockSpec(memory_space=pl.ANY), vmem, pl.BlockSpec(memory_space=pltpu.SMEM), vmem],
+            out_specs=vmem,
+            scratch_shapes=scratch(slots),
+            compiler_params=pltpu.CompilerParams(
+                collective_id=blocks - slots, has_side_effects=True, vmem_limit_bytes=62 * 2**20),
+            name="spod",
+        )
+
+    args = (pressure, cell_weight.reshape(blocks, LANES), live_cells, mode_order.reshape(1, modes))
+    if adaptive:
+        count = jnp.maximum((live_cells + (LANES - 1)) // LANES, floor)
+        low = blocks - 2
+        code = jnp.sum(count + 256 * (count <= floor) + 4096 * (count > low) + 65536 * (count > low + 1))
+        total, short = code % 256, code // 256 % 16
+        over, more = code // 4096 % 16, code // 65536
+        tight = jnp.logical_and(total <= low * n_grp, jnp.logical_or(short <= over, more == 0))
+        pick = jnp.where(tight, 2, jnp.where(total <= (low + 1) * n_grp, 1, 0))
+        packed = lax.switch(pick, [call(blocks), call(blocks - 1), call(blocks - 2)], *args)
+    else:
+        packed = call(blocks)(*args)
     out = packed.reshape(modes // pack // n_sec, part, pack, snaps)
     return out.transpose(0, 2, 1, 3).reshape(modes // n_sec, part, snaps)
 

time: 202 us -> 172 us (0.85)
  Pallas kernels: 200 us -> 166 us
  between operations: 0.02 us -> 2.7 us
    pallas_call x1, Pallas kernels: 200 us -> 166 us  [on_device(): lax.switch(pick, [call(blocks), call(blocks - 1), call(blocks - 2)], *args)]
where the time goes in v1:
time: 172 us; the launch traced here: 171 us
  Pallas kernels  166 us (97%)
  between operations  2.7 us (2%)
    pallas_call x1, Pallas kernels, on_device(): lax.switch(pick, [call(blocks), call(blocks - 1), call(blocks - 2)], *args)  166 us

profile of v1, /device:TPU:0, one launch (start us, length us, event | category | flops | bytes accessed | tf_op | source)
XLA Modules:
  0.0 171.4 jit_solution(11613433761891233223)
XLA Ops:
  0.0 1.3 fusion.3
  4.0 166.6 %conditional.1 = (f32[32,128]{1,0:T(8,128)S(1)}) conditional(s32[]{:T(128)} %clamp.3, (f32[32,64,1024]{2,1,0:T(8,128)}, f32[8,128]{1,0:T(8,128)}, s32[8]{0:T(128)}, s32[1,128]{1,0:T(1,128)}) %tuple.21, (f32[32,64,1024]{2,1,0:T(8,128)}, f32[8,128]{1,0:T(8,128)}, s32[8]{0:T(128)}, s32[1,128]{1,0:T(1,128)}) %tuple.22, ...), branch_computations={%region_1.2_spmd, %region_2.3_spmd, %region_3.4_spmd} | conditional | bytes 8 | solution.py:761
  4.2 166.1 %spod.5 = f32[32,128]{1,0:T(8,128)S(1)} custom-call(f32[32,64,1024]{2,1,0:T(8,128)} %get-tuple-element.41.refs_0_, f32[8,128]{1,0:T(8,128)} %get-tuple-element.42.refs_1_, s32[8]{0:T(128)} %get-tuple-element.43.refs_2_, s32[1,128]{1,0:T(1,128)} %get-tuple-element.44.refs_3_), custom_call_target="tpu_custom_call" | custom-call | tf_op jit(solution)/shard_map/cond/branch_2_fun/spod/pallas_call | solution.py:761
  170.6 0.1 reshape.14
  170.7 0.6 copy.5
